TPU v7x, 256 devices: a whole 4x4x8 slice. The times are simulated.
256 devices in a mesh: panel: 2 (over core), ang: 32 (over z, x), rad: 4 (over y).
Axes of the slice: x: 4, y: 4, z: 8, core: 2. Of those that a mesh axis runs over, the one named last changes fastest.
Arguments:
- density: float32 [2, 8, 512, 512], P('panel', 'rad', 'ang'), may hold values from 1 to 2
- momentum: float32 [2, 3, 8, 512, 512], P('panel', None, 'rad', 'ang'), may hold values from -2.5 to 2.5
- magnetic: float32 [2, 3, 8, 512, 512], P('panel', None, 'rad', 'ang'), may hold values from -2.5 to 2.5
- partner_device: int32 [2, 1024, 1], P('panel', 'ang'), may hold values from 0 to 31; in each aligned block of 32 rows (0 to 31, 32 to 63, ..., all dimensions but the last counted through in order) at most 2 rows name the same one
- partner_phi: int32 [2, 1024], P('panel', 'ang'), may hold values from 0 to 14
- partner_theta: int32 [2, 1024], P('panel', 'ang'), may hold values from 0 to 510
- partner_weight: float32 [2, 1024, 4], P('panel', 'ang'), may hold values from 0 to 1, as said below
- border_turn: float32 [2, 1024], P('panel', 'ang'), may hold values from -3.140625 to 3.140625
Outputs:
- density_next: float32 [2, 8, 512, 512], P('panel', 'rad', 'ang')
- momentum_next: float32 [2, 3, 8, 512, 512], P('panel', None, 'rad', 'ang')
- magnetic_next: float32 [2, 3, 8, 512, 512], P('panel', None, 'rad', 'ang')
Inputs may be any that keep to these rules, and one draw needn't show every extreme that they name: `partner_device`: within the 32 table rows of one device (aligned blocks), at most 2 rows name the same source device. `partner_weight`: each row's weights are (1-u)(1-v), (1-u)v, u(1-v), uv for some u, v in [0, 1].
All inputs are finite; a program needn't handle non-finite values.
Results may differ from a plain program's by a relative error of at most 0.00005.
Values sent between devices are 32-bit elements; how exact they have to be, the bound alone decides.
No kernel may reach another device: no remote copies, remote signals or barrier semaphores. Data moves between devices by JAX's collectives and lax.ppermute only.
A program may use at most 64 MiB of HBM per device.

v0:
```python
import math
import jax
import jax.numpy as jnp
from jax import lax
from jax.sharding import PartitionSpec as P

time_step = 0.15
sound_sq = 1.0
viscosity = 0.1
resistivity = 0.1
r_inner = 0.35


def swapped(block, axis, apart):
    count = lax.axis_size(axis)
    route = []
    for low in range(count):
        high = low | 1 << apart
        if high != low and high < count:
            route += [(low, high), (high, low)]
    return lax.ppermute(block, axis, route)


def padded(value, sides, width):
    for axis, dim in sides:
        size, length = (lax.axis_size(axis), value.shape[dim])
        up = [(i, (i + 1) % size) for i in range(size - 1)]
        down = [(j, i) for i, j in up]
        last = lax.slice_in_dim(value, length - width, length, axis=dim)
        first = lax.slice_in_dim(value, 0, width, axis=dim)
        before = lax.ppermute(last, axis, up)
        after = lax.ppermute(first, axis, down)
        value = jnp.concatenate([before, value, after], axis=dim)
    return value


def field_of(block, index):
    return block[..., index, :, :, :]


def fluxes(block, direction):
    mass_field = field_of(block, 0)
    moment = [field_of(block, 1 + component) for component in range(3)]
    magnet = [field_of(block, 4 + component) for component in range(3)]
    velocity = [moment[component] / mass_field for component in range(3)]
    pressure = sound_sq * mass_field + 0.5 * (
        magnet[0] * magnet[0] + magnet[1] * magnet[1] + magnet[2] * magnet[2]
    )
    pieces = [moment[direction]]
    for component in range(3):
        flux_term = moment[component] * velocity[direction] - magnet[component] * magnet[direction]
        if component == direction:
            flux_term = flux_term + pressure
        pieces.append(flux_term)
    for component in range(3):
        pieces.append(
            velocity[direction] * magnet[component] - magnet[direction] * velocity[component]
        )
    return jnp.stack(pieces, axis=-4)


def tendency(current, radial, polar, azimuth, half_t, half_p, sq_t, sq_p):
    flux_r = fluxes(radial, 0)
    flux_t = fluxes(polar, 1)
    flux_p = fluxes(azimuth, 2)
    divergence = (flux_r[..., 2:, :, :] - flux_r[..., :-2, :, :]) * 0.5
    divergence = divergence + (flux_t[..., 2:] - flux_t[..., :-2]) * half_t
    divergence = divergence + (flux_p[..., :, 2:, :] - flux_p[..., :, :-2, :]) * half_p
    laplace_sum = radial[..., 2:, :, :] - 2.0 * current + radial[..., :-2, :, :]
    laplace_sum = laplace_sum + (polar[..., 2:] - 2.0 * current + polar[..., :-2]) * sq_t
    laplace_sum = (
        laplace_sum + (azimuth[..., :, 2:, :] - 2.0 * current + azimuth[..., :, :-2, :]) * sq_p
    )
    mixing = jnp.array(
        [0.0, viscosity, viscosity, viscosity, resistivity, resistivity, resistivity], jnp.float32
    ).reshape(7, 1, 1, 1)
    return mixing * laplace_sum - divergence


def turn_frame(ghost, cosine, sine):
    pieces = [ghost[0], ghost[1]]
    pieces.append(cosine * ghost[2] + sine * ghost[3])
    pieces.append(cosine * ghost[3] - sine * ghost[2])
    pieces.append(ghost[4])
    pieces.append(cosine * ghost[5] + sine * ghost[6])
    pieces.append(cosine * ghost[6] - sine * ghost[5])
    return jnp.stack(pieces, axis=0)


def route_request(packed):
    crossed = swapped(packed, "panel", 0)
    return lax.all_to_all(crossed, "ang", split_axis=0, concat_axis=0, tiled=True)


def route_reply(answer):
    crossed = swapped(answer, "panel", 0)
    return lax.all_to_all(crossed, "ang", split_axis=1, concat_axis=1, tiled=True)


def body(
    density,
    momentum,
    magnetic,
    partner_device,
    partner_phi,
    partner_theta,
    partner_weight,
    border_turn,
):
    fields_now = jnp.concatenate([density, momentum[0], magnetic[0]], axis=0)
    fields, rows_r, rows_p, rows_t = fields_now.shape
    n_ang = lax.axis_size("ang")
    n_rad = lax.axis_size("rad")
    border = partner_phi.shape[1]
    capacity = max(2, 2 * border // n_ang)
    slot_count = n_ang * capacity
    stacked_rows = fields * rows_r
    highest = lax.Precision.HIGHEST
    level = lax.axis_index("rad") * rows_r + jnp.arange(rows_r, dtype=jnp.int32)
    radius = r_inner + (level.astype(jnp.float32) + 0.5) * ((1.0 - r_inner) / (rows_r * n_rad))
    colatitude = math.pi / 4 + (jnp.arange(rows_t).astype(jnp.float32) + 0.5) * (
        math.pi / 2 / rows_t
    )
    inv_radius = (1.0 / radius).reshape(rows_r, 1, 1)
    inv_both = inv_radius / jnp.sin(colatitude)
    half_t = 0.5 * inv_radius
    half_p = 0.5 * inv_both
    sq_t = inv_radius * inv_radius
    sq_p = inv_both * inv_both
    mirror = jnp.array([1.0, -1.0, -1.0, -1.0, 1.0, 1.0, 1.0], jnp.float32).reshape(7, 1, 1, 1)
    first_r = lax.axis_index("rad") == 0
    last_r = lax.axis_index("rad") == n_rad - 1
    first_p = lax.axis_index("ang") == 0
    last_p = lax.axis_index("ang") == n_ang - 1
    source_ang = partner_device[0, :, 0]
    one_hot = (source_ang[:, None] == jnp.arange(n_ang, dtype=jnp.int32)[None, :]).astype(jnp.int32)
    ranked = jnp.sum(one_hot * (jnp.cumsum(one_hot, axis=0) - 1), axis=1)
    target_slot = source_ang * capacity + ranked
    placing = (jnp.arange(slot_count, dtype=jnp.int32)[:, None] == target_slot[None, :]).astype(
        jnp.float32
    )
    base_cell = (partner_phi[0] * rows_t + partner_theta[0]).astype(jnp.float32)
    weights = partner_weight[0]
    payload = base_cell[:, None]
    packed = jnp.dot(placing, payload, precision=highest).reshape(n_ang, capacity, payload.shape[1])
    asked = route_request(packed)
    cell_index = (asked[:, :, 0].reshape(slot_count) + 0.5).astype(jnp.int32)
    offsets = jnp.array([0, 1, rows_t, rows_t + 1], jnp.int32)
    gather_index = (cell_index[:, None] + offsets[None, :]).reshape(slot_count * 4)
    cosine = jnp.cos(border_turn[0])
    sine = jnp.sin(border_turn[0])

    def overset(current):
        table = current.reshape(stacked_rows, rows_p * rows_t)
        corner = jnp.take(table, gather_index, axis=1).reshape(stacked_rows, slot_count, 4)
        returned = route_reply(corner.reshape(stacked_rows, n_ang, capacity, 4)).reshape(
            stacked_rows, slot_count, 4
        )
        picked = [jnp.dot(returned[:, :, index], placing, precision=highest) for index in range(4)]
        ghost = weights[:, 0] * picked[0] + weights[:, 1] * picked[1]
        ghost = ghost + weights[:, 2] * picked[2]
        ghost = ghost + weights[:, 3] * picked[3]
        ghost = turn_frame(ghost.reshape(fields, rows_r, border), cosine, sine)
        return (ghost[:, :, :rows_p], ghost[:, :, rows_p:])

    def evaluate(current):
        haloed = padded(current, (("ang", 2), ("rad", 1)), 1)
        lower_r = jnp.where(first_r, mirror * current[:, :1], haloed[:, :1, 1:-1])
        upper_r = jnp.where(last_r, mirror * current[:, -1:], haloed[:, -1:, 1:-1])
        lower_p = jnp.where(first_p, mirror * current[:, :, :1], haloed[:, 1:-1, :1])
        upper_p = jnp.where(last_p, mirror * current[:, :, -1:], haloed[:, 1:-1, -1:])
        radial = jnp.concatenate([lower_r, current, upper_r], axis=1)
        azimuth = jnp.concatenate([lower_p, current, upper_p], axis=2)
        lower_t, upper_t = overset(current)
        polar = jnp.concatenate([lower_t[..., None], current, upper_t[..., None]], axis=3)
        return tendency(current, radial, polar, azimuth, half_t, half_p, sq_t, sq_p)

    slope_one = evaluate(fields_now)
    slope_two = evaluate(fields_now + 0.5 * time_step * slope_one)
    slope_three = evaluate(fields_now + 0.5 * time_step * slope_two)
    slope_four = evaluate(fields_now + time_step * slope_three)
    updated = fields_now + time_step / 6.0 * (
        slope_one + 2.0 * slope_two + 2.0 * slope_three + slope_four
    )
    return (updated[0:1], updated[1:4][None], updated[4:7][None])


def solution(mesh):
    in_specs = (
        P("panel", "rad", "ang", None),
        P("panel", None, "rad", "ang", None),
        P("panel", None, "rad", "ang", None),
        P("panel", "ang", None),
        P("panel", "ang"),
        P("panel", "ang"),
        P("panel", "ang", None),
        P("panel", "ang"),
    )
    out_specs = (
        P("panel", "rad", "ang", None),
        P("panel", None, "rad", "ang", None),
        P("panel", None, "rad", "ang", None),
    )
    return jax.shard_map(body, mesh=mesh, in_specs=in_specs, out_specs=out_specs, check_vma=False)
```

profile of v0, /device:TPU:2, one launch (start us, length us, event | category | flops | bytes accessed | tf_op | source)
XLA Modules:
  0.0 199.3 jit_solution(3785506237722466291)
XLA Ops:
  1.8 4.3 %collective-permute-start.1 = (f32[7,2,1,512]{3,2,1,0:T(1,128)S(1)}, f32[7,2,1,512]{3,2,1,0:T(1,128)S(1)}, u32[]{:S(2)}, u32[]{:S(2)}) collective-permute-start(f32[7,2,1,512]{3,2,1,0:T(1,128)S(1)} %get-tuple-element.75), channel_id=1, source_target_pairs={{4,0},{8,4},{12,8},{16,12},{20,16},{24,20},{28,24},{32,28},{36,32}... | collective-permute-start | bytes 86024 | tf_op jit(solution)/shard_map/ppermute | solution.py:32
  13.2 13.2 %all-to-all-start = ((f32[32,2,1]{1,2,0:T(1,128)}), f32[32,2,1]{1,2,0:T(1,128)S(1)}, u32[]{:S(2)}, u32[]{:S(2)}) async-start(f32[32,2,1]{1,2,0:T(1,128)} %copy.59), calls=%async_computation | async-start | bytes 32768 | tf_op jit(solution)/shard_map/all_to_all | solution.py:92
  27.5 2.7 %copy.60 = f32[14,8192]{0,1:T(8,128)} copy(f32[14,8192]{1,0:T(8,128)S(1)} %bitcast.210) | data formatting | bytes 917504 | tf_op jit(solution)/shard_map/reshape | solution.py:154
  30.2 4.7 %all-to-all-done = f32[32,2,1]{1,2,0:T(1,128)S(1)} async-done(((f32[32,2,1]{1,2,0:T(1,128)}), f32[32,2,1]{1,2,0:T(1,128)S(1)}, u32[]{:S(2)}, u32[]{:S(2)}) %all-to-all-start) | async-done | bytes 288 | tf_op jit(solution)/shard_map/all_to_all | solution.py:92
  35.3 2.9 %gather_fusion = f32[256,14]{1,0:T(8,128)S(1)} fusion(f32[14,8192]{0,1:T(8,128)} %copy.60, s32[1024]{0:T(1024)S(1)} %pad_clamp_fusion), kind=kCustom, calls=%fused_computation.clone | custom fusion | bytes 29696 | tf_op jit(solution)/shard_map/jit(_take)/gather | solution.py:155
  39.9 5.1 %all-to-all-start.1 = ((f32[14,32,2,4]{0,3,2,1:T(4,128)}), f32[14,32,2,4]{0,3,2,1:T(4,128)S(1)}, u32[]{:S(2)}, u32[]{:S(2)}) async-start(f32[14,32,2,4]{0,3,2,1:T(4,128)} %collective-permute-done.5), calls=%async_computation.1 | async-start | bytes 262144 | tf_op jit(solution)/shard_map/all_to_all | solution.py:97
  46.4 4.2 %collective-permute-start.3 = (f32[7,1,18,512]{3,2,1,0:T(8,128)}, f32[7,1,18,512]{3,2,1,0:T(8,128)}, u32[]{:S(2)}, u32[]{:S(2)}) collective-permute-start(f32[7,1,18,512]{3,2,1,0:T(8,128)} %get-tuple-element.40), channel_id=1, source_target_pairs={{0,1},{1,2},{2,3},{4,5},{5,6},{6,7},{8,9},{9,10},{10,11},{12,13},{... | collective-permute-start | bytes 774152 | tf_op jit(solution)/shard_map/ppermute | solution.py:31
  57.4 4.6 %collective-permute-done.2 = f32[7,1,18,512]{3,2,1,0:T(8,128)} collective-permute-done((f32[7,1,18,512]{3,2,1,0:T(8,128)S(1)}, f32[7,1,18,512]{3,2,1,0:T(8,128)}, u32[]{:S(2)}, u32[]{:S(2)}) %collective-permute-start.2) | collective-permute-done | bytes 258080 | tf_op jit(solution)/shard_map/ppermute | solution.py:32
  67.0 3.3 %collective-permute-start.6 = (f32[7,2,1,512]{3,2,1,0:T(1,128)S(1)}, f32[7,2,1,512]{3,2,1,0:T(1,128)S(1)}, u32[]{:S(2)}, u32[]{:S(2)}) collective-permute-start(f32[7,2,1,512]{3,2,1,0:T(1,128)S(1)} %get-tuple-element.70), channel_id=1, source_target_pairs={{0,4},{4,8},{8,12},{12,16},{16,20},{20,24},{24,28},{28,32},{32,36}... | collective-permute-start | bytes 86024 | tf_op jit(solution)/shard_map/ppermute | solution.py:31
  73.3 2.9 %gather_fusion.1 = f32[256,14]{1,0:T(8,128)S(1)} fusion(f32[14,8192]{0,1:T(8,128)} %copy.65, s32[1024]{0:T(1024)S(1)} %pad_clamp_fusion), kind=kCustom, calls=%fused_computation.1.clone | custom fusion | bytes 29696 | tf_op jit(solution)/shard_map/jit(_take)/gather | solution.py:155
  77.9 11.7 %all-to-all-start.2 = ((f32[14,32,2,4]{0,3,2,1:T(4,128)}), f32[14,32,2,4]{0,3,2,1:T(4,128)S(1)}, u32[]{:S(2)}, u32[]{:S(2)}) async-start(f32[14,32,2,4]{0,3,2,1:T(4,128)} %collective-permute-done.10), calls=%async_computation.2 | async-start | bytes 262144 | tf_op jit(solution)/shard_map/all_to_all | solution.py:97
  91.2 3.5 %collective-permute-start.9 = (f32[7,1,18,512]{3,2,1,0:T(8,128)}, f32[7,1,18,512]{3,2,1,0:T(8,128)}, u32[]{:S(2)}, u32[]{:S(2)}) collective-permute-start(f32[7,1,18,512]{3,2,1,0:T(8,128)} %get-tuple-element.38), channel_id=1, source_target_pairs={{0,1},{1,2},{2,3},{4,5},{5,6},{6,7},{8,9},{9,10},{10,11},{12,13},{... | collective-permute-start | bytes 774152 | tf_op jit(solution)/shard_map/ppermute | solution.py:31
  96.0 2.8 %all-to-all-done.2 = f32[14,32,2,4]{0,3,2,1:T(4,128)S(1)} async-done(((f32[14,32,2,4]{0,3,2,1:T(4,128)}), f32[14,32,2,4]{0,3,2,1:T(4,128)S(1)}, u32[]{:S(2)}, u32[]{:S(2)}) %all-to-all-start.2) | async-done | bytes 14368 | tf_op jit(solution)/shard_map/all_to_all | solution.py:97
  101.3 4.8 %collective-permute-done.8 = f32[7,1,18,512]{3,2,1,0:T(8,128)} collective-permute-done((f32[7,1,18,512]{3,2,1,0:T(8,128)}, f32[7,1,18,512]{3,2,1,0:T(8,128)}, u32[]{:S(2)}, u32[]{:S(2)}) %collective-permute-start.8) | collective-permute-done | bytes 258080 | tf_op jit(solution)/shard_map/ppermute | solution.py:32
  112.3 3.6 %collective-permute-start.11 = (f32[7,2,1,512]{3,2,1,0:T(1,128)S(1)}, f32[7,2,1,512]{3,2,1,0:T(1,128)S(1)}, u32[]{:S(2)}, u32[]{:S(2)}) collective-permute-start(f32[7,2,1,512]{3,2,1,0:T(1,128)S(1)} %get-tuple-element.66), channel_id=1, source_target_pairs={{0,4},{4,8},{8,12},{12,16},{16,20},{20,24},{24,28},{28,32},{32,36}... | collective-permute-start | bytes 86024 | tf_op jit(solution)/shard_map/ppermute | solution.py:31
  119.0 2.9 %gather_fusion.2 = f32[256,14]{1,0:T(8,128)S(1)} fusion(f32[14,8192]{0,1:T(8,128)} %copy.70, s32[1024]{0:T(1024)S(1)} %pad_clamp_fusion), kind=kCustom, calls=%fused_computation.2.clone | custom fusion | bytes 29696 | tf_op jit(solution)/shard_map/jit(_take)/gather | solution.py:155
  123.5 11.6 %all-to-all-start.3 = ((f32[14,32,2,4]{0,3,2,1:T(4,128)}), f32[14,32,2,4]{0,3,2,1:T(4,128)S(1)}, u32[]{:S(2)}, u32[]{:S(2)}) async-start(f32[14,32,2,4]{0,3,2,1:T(4,128)} %collective-permute-done.15), calls=%async_computation.3 | async-start | bytes 262144 | tf_op jit(solution)/shard_map/all_to_all | solution.py:97
  137.5 3.2 %collective-permute-start.14 = (f32[7,1,18,512]{3,2,1,0:T(8,128)}, f32[7,1,18,512]{3,2,1,0:T(8,128)}, u32[]{:S(2)}, u32[]{:S(2)}) collective-permute-start(f32[7,1,18,512]{3,2,1,0:T(8,128)} %get-tuple-element.36), channel_id=1, source_target_pairs={{0,1},{1,2},{2,3},{4,5},{5,6},{6,7},{8,9},{9,10},{10,11},{12,13},{... | collective-permute-start | bytes 774152 | tf_op jit(solution)/shard_map/ppermute | solution.py:31
  147.3 4.6 %collective-permute-done.13 = f32[7,1,18,512]{3,2,1,0:T(8,128)} collective-permute-done((f32[7,1,18,512]{3,2,1,0:T(8,128)S(1)}, f32[7,1,18,512]{3,2,1,0:T(8,128)}, u32[]{:S(2)}, u32[]{:S(2)}) %collective-permute-start.13) | collective-permute-done | bytes 258080 | tf_op jit(solution)/shard_map/ppermute | solution.py:32
  156.7 3.4 %collective-permute-start.16 = (f32[7,2,1,512]{3,2,1,0:T(1,128)S(1)}, f32[7,2,1,512]{3,2,1,0:T(1,128)S(1)}, u32[]{:S(2)}, u32[]{:S(2)}) collective-permute-start(f32[7,2,1,512]{3,2,1,0:T(1,128)S(1)} %get-tuple-element.62), channel_id=1, source_target_pairs={{0,4},{4,8},{8,12},{12,16},{16,20},{20,24},{24,28},{28,32},{32,36}... | collective-permute-start | bytes 86024 | tf_op jit(solution)/shard_map/ppermute | solution.py:31
  163.2 2.9 %gather_fusion.3 = f32[256,14]{1,0:T(8,128)S(1)} fusion(f32[14,8192]{0,1:T(8,128)} %copy.75, s32[1024]{0:T(1024)S(1)} %pad_clamp_fusion), kind=kCustom, calls=%fused_computation.3.clone | custom fusion | bytes 29696 | tf_op jit(solution)/shard_map/jit(_take)/gather | solution.py:155
  167.8 11.6 %all-to-all-start.4 = ((f32[14,32,2,4]{0,3,2,1:T(4,128)}), f32[14,32,2,4]{0,3,2,1:T(4,128)S(1)}, u32[]{:S(2)}, u32[]{:S(2)}) async-start(f32[14,32,2,4]{0,3,2,1:T(4,128)} %collective-permute-done.20), calls=%async_computation.4 | async-start | bytes 262144 | tf_op jit(solution)/shard_map/all_to_all | solution.py:97
  185.2 3.2 %all-to-all-done.4 = f32[14,32,2,4]{0,3,2,1:T(4,128)S(1)} async-done(((f32[14,32,2,4]{0,3,2,1:T(4,128)}), f32[14,32,2,4]{0,3,2,1:T(4,128)S(1)}, u32[]{:S(2)}, u32[]{:S(2)}) %all-to-all-start.4) | async-done | bytes 14368 | tf_op jit(solution)/shard_map/all_to_all | solution.py:97
  190.7 4.6 %collective-permute-done.18 = f32[7,1,18,512]{3,2,1,0:T(8,128)} collective-permute-done((f32[7,1,18,512]{3,2,1,0:T(8,128)S(1)}, f32[7,1,18,512]{3,2,1,0:T(8,128)}, u32[]{:S(2)}, u32[]{:S(2)}) %collective-permute-start.18) | collective-permute-done | bytes 258080 | tf_op jit(solution)/shard_map/ppermute | solution.py:32
  (270 shorter events, 74.9 us)
Async XLA Ops:
  1.8 43.1 %collective-permute-start.1 = (f32[7,2,1,512]{3,2,1,0:T(1,128)S(1)}, f32[7,2,1,512]{3,2,1,0:T(1,128)S(1)}, u32[]{:S(2)}, u32[]{:S(2)}) collective-permute-start(f32[7,2,1,512]{3,2,1,0:T(1,128)S(1)} %get-tuple-element.75), channel_id=1, source_target_pairs={{4,0},{8,4},{12,8},{16,12},{20,16},{24,20},{28,24},{32,28},{36,32}... | collective-permute-start | bytes 86024 | tf_op jit(solution)/shard_map/ppermute | solution.py:32
  6.1 38.8 %collective-permute-start = (f32[7,2,1,512]{3,2,1,0:T(1,128)S(1)}, f32[7,2,1,512]{3,2,1,0:T(1,128)S(1)}, u32[]{:S(2)}, u32[]{:S(2)}) collective-permute-start(f32[7,2,1,512]{3,2,1,0:T(1,128)S(1)} %get-tuple-element.74), channel_id=1, source_target_pairs={{0,4},{4,8},{8,12},{12,16},{16,20},{20,24},{24,28},{28,32},{32,36}... | collective-permute-start | bytes 86024 | tf_op jit(solution)/shard_map/ppermute | solution.py:31
  13.2 21.7 %all-to-all-start = ((f32[32,2,1]{1,2,0:T(1,128)}), f32[32,2,1]{1,2,0:T(1,128)S(1)}, u32[]{:S(2)}, u32[]{:S(2)}) async-start(f32[32,2,1]{1,2,0:T(1,128)} %copy.59), calls=%async_computation | async-start | bytes 32768 | tf_op jit(solution)/shard_map/all_to_all | solution.py:92
  38.3 1.6 collective-permute-start.5
  39.9 14.2 %all-to-all-start.1 = ((f32[14,32,2,4]{0,3,2,1:T(4,128)}), f32[14,32,2,4]{0,3,2,1:T(4,128)S(1)}, u32[]{:S(2)}, u32[]{:S(2)}) async-start(f32[14,32,2,4]{0,3,2,1:T(4,128)} %collective-permute-done.5), calls=%async_computation.1 | async-start | bytes 262144 | tf_op jit(solution)/shard_map/all_to_all | solution.py:97
  46.4 11.0 %collective-permute-start.3 = (f32[7,1,18,512]{3,2,1,0:T(8,128)}, f32[7,1,18,512]{3,2,1,0:T(8,128)}, u32[]{:S(2)}, u32[]{:S(2)}) collective-permute-start(f32[7,1,18,512]{3,2,1,0:T(8,128)} %get-tuple-element.40), channel_id=1, source_target_pairs={{0,1},{1,2},{2,3},{4,5},{5,6},{6,7},{8,9},{9,10},{10,11},{12,13},{... | collective-permute-start | bytes 774152 | tf_op jit(solution)/shard_map/ppermute | solution.py:31
  50.6 11.4 %collective-permute-start.2 = (f32[7,1,18,512]{3,2,1,0:T(8,128)S(1)}, f32[7,1,18,512]{3,2,1,0:T(8,128)}, u32[]{:S(2)}, u32[]{:S(2)}) collective-permute-start(f32[7,1,18,512]{3,2,1,0:T(8,128)S(1)} %get-tuple-element.41), channel_id=1, source_target_pairs={{1,0},{2,1},{3,2},{5,4},{6,5},{7,6},{9,8},{10,9},{11,10},{13,12},{... | collective-permute-start | bytes 774152 | tf_op jit(solution)/shard_map/ppermute | solution.py:32
  64.4 25.2 %collective-permute-start.7 = (f32[7,2,1,512]{3,2,1,0:T(1,128)S(1)}, f32[7,2,1,512]{3,2,1,0:T(1,128)S(1)}, u32[]{:S(2)}, u32[]{:S(2)}) collective-permute-start(f32[7,2,1,512]{3,2,1,0:T(1,128)S(1)} %get-tuple-element.71), channel_id=1, source_target_pairs={{4,0},{8,4},{12,8},{16,12},{20,16},{24,20},{28,24},{32,28},{36,32}... | collective-permute-start | bytes 86024 | tf_op jit(solution)/shard_map/ppermute | solution.py:32
  67.0 22.7 %collective-permute-start.6 = (f32[7,2,1,512]{3,2,1,0:T(1,128)S(1)}, f32[7,2,1,512]{3,2,1,0:T(1,128)S(1)}, u32[]{:S(2)}, u32[]{:S(2)}) collective-permute-start(f32[7,2,1,512]{3,2,1,0:T(1,128)S(1)} %get-tuple-element.70), channel_id=1, source_target_pairs={{0,4},{4,8},{8,12},{12,16},{16,20},{20,24},{24,28},{28,32},{32,36}... | collective-permute-start | bytes 86024 | tf_op jit(solution)/shard_map/ppermute | solution.py:31
  76.4 1.6 collective-permute-start.10
  77.9 20.8 %all-to-all-start.2 = ((f32[14,32,2,4]{0,3,2,1:T(4,128)}), f32[14,32,2,4]{0,3,2,1:T(4,128)S(1)}, u32[]{:S(2)}, u32[]{:S(2)}) async-start(f32[14,32,2,4]{0,3,2,1:T(4,128)} %collective-permute-done.10), calls=%async_computation.2 | async-start | bytes 262144 | tf_op jit(solution)/shard_map/all_to_all | solution.py:97
  91.2 10.1 %collective-permute-start.9 = (f32[7,1,18,512]{3,2,1,0:T(8,128)}, f32[7,1,18,512]{3,2,1,0:T(8,128)}, u32[]{:S(2)}, u32[]{:S(2)}) collective-permute-start(f32[7,1,18,512]{3,2,1,0:T(8,128)} %get-tuple-element.38), channel_id=1, source_target_pairs={{0,1},{1,2},{2,3},{4,5},{5,6},{6,7},{8,9},{9,10},{10,11},{12,13},{... | collective-permute-start | bytes 774152 | tf_op jit(solution)/shard_map/ppermute | solution.py:31
  94.7 11.5 %collective-permute-start.8 = (f32[7,1,18,512]{3,2,1,0:T(8,128)}, f32[7,1,18,512]{3,2,1,0:T(8,128)}, u32[]{:S(2)}, u32[]{:S(2)}) collective-permute-start(f32[7,1,18,512]{3,2,1,0:T(8,128)} %get-tuple-element.39), channel_id=1, source_target_pairs={{1,0},{2,1},{3,2},{5,4},{6,5},{7,6},{9,8},{10,9},{11,10},{13,12},{... | collective-permute-start | bytes 774152 | tf_op jit(solution)/shard_map/ppermute | solution.py:32
  109.9 25.3 %collective-permute-start.12 = (f32[7,2,1,512]{3,2,1,0:T(1,128)S(1)}, f32[7,2,1,512]{3,2,1,0:T(1,128)S(1)}, u32[]{:S(2)}, u32[]{:S(2)}) collective-permute-start(f32[7,2,1,512]{3,2,1,0:T(1,128)S(1)} %get-tuple-element.67), channel_id=1, source_target_pairs={{4,0},{8,4},{12,8},{16,12},{20,16},{24,20},{28,24},{32,28},{36,32}... | collective-permute-start | bytes 86024 | tf_op jit(solution)/shard_map/ppermute | solution.py:32
  112.3 22.9 %collective-permute-start.11 = (f32[7,2,1,512]{3,2,1,0:T(1,128)S(1)}, f32[7,2,1,512]{3,2,1,0:T(1,128)S(1)}, u32[]{:S(2)}, u32[]{:S(2)}) collective-permute-start(f32[7,2,1,512]{3,2,1,0:T(1,128)S(1)} %get-tuple-element.66), channel_id=1, source_target_pairs={{0,4},{4,8},{8,12},{12,16},{16,20},{20,24},{24,28},{28,32},{32,36}... | collective-permute-start | bytes 86024 | tf_op jit(solution)/shard_map/ppermute | solution.py:31
  122.0 1.6 collective-permute-start.15
  123.5 20.7 %all-to-all-start.3 = ((f32[14,32,2,4]{0,3,2,1:T(4,128)}), f32[14,32,2,4]{0,3,2,1:T(4,128)S(1)}, u32[]{:S(2)}, u32[]{:S(2)}) async-start(f32[14,32,2,4]{0,3,2,1:T(4,128)} %collective-permute-done.15), calls=%async_computation.3 | async-start | bytes 262144 | tf_op jit(solution)/shard_map/all_to_all | solution.py:97
  137.5 9.8 %collective-permute-start.14 = (f32[7,1,18,512]{3,2,1,0:T(8,128)}, f32[7,1,18,512]{3,2,1,0:T(8,128)}, u32[]{:S(2)}, u32[]{:S(2)}) collective-permute-start(f32[7,1,18,512]{3,2,1,0:T(8,128)} %get-tuple-element.36), channel_id=1, source_target_pairs={{0,1},{1,2},{2,3},{4,5},{5,6},{6,7},{8,9},{9,10},{10,11},{12,13},{... | collective-permute-start | bytes 774152 | tf_op jit(solution)/shard_map/ppermute | solution.py:31
  140.7 11.3 %collective-permute-start.13 = (f32[7,1,18,512]{3,2,1,0:T(8,128)S(1)}, f32[7,1,18,512]{3,2,1,0:T(8,128)}, u32[]{:S(2)}, u32[]{:S(2)}) collective-permute-start(f32[7,1,18,512]{3,2,1,0:T(8,128)S(1)} %get-tuple-element.37), channel_id=1, source_target_pairs={{1,0},{2,1},{3,2},{5,4},{6,5},{7,6},{9,8},{10,9},{11,10},{13,12},{... | collective-permute-start | bytes 774152 | tf_op jit(solution)/shard_map/ppermute | solution.py:32
  154.3 25.1 %collective-permute-start.17 = (f32[7,2,1,512]{3,2,1,0:T(1,128)S(1)}, f32[7,2,1,512]{3,2,1,0:T(1,128)S(1)}, u32[]{:S(2)}, u32[]{:S(2)}) collective-permute-start(f32[7,2,1,512]{3,2,1,0:T(1,128)S(1)} %get-tuple-element.63), channel_id=1, source_target_pairs={{4,0},{8,4},{12,8},{16,12},{20,16},{24,20},{28,24},{32,28},{36,32}... | collective-permute-start | bytes 86024 | tf_op jit(solution)/shard_map/ppermute | solution.py:32
  156.7 22.7 %collective-permute-start.16 = (f32[7,2,1,512]{3,2,1,0:T(1,128)S(1)}, f32[7,2,1,512]{3,2,1,0:T(1,128)S(1)}, u32[]{:S(2)}, u32[]{:S(2)}) collective-permute-start(f32[7,2,1,512]{3,2,1,0:T(1,128)S(1)} %get-tuple-element.62), channel_id=1, source_target_pairs={{0,4},{4,8},{8,12},{12,16},{16,20},{20,24},{24,28},{28,32},{32,36}... | collective-permute-start | bytes 86024 | tf_op jit(solution)/shard_map/ppermute | solution.py:31
  167.8 20.7 %all-to-all-start.4 = ((f32[14,32,2,4]{0,3,2,1:T(4,128)}), f32[14,32,2,4]{0,3,2,1:T(4,128)S(1)}, u32[]{:S(2)}, u32[]{:S(2)}) async-start(f32[14,32,2,4]{0,3,2,1:T(4,128)} %collective-permute-done.20), calls=%async_computation.4 | async-start | bytes 262144 | tf_op jit(solution)/shard_map/all_to_all | solution.py:97
  181.7 8.9 %collective-permute-start.19 = (f32[7,1,18,512]{3,2,1,0:T(8,128)}, f32[7,1,18,512]{3,2,1,0:T(8,128)}, u32[]{:S(2)}, u32[]{:S(2)}) collective-permute-start(f32[7,1,18,512]{3,2,1,0:T(8,128)} %get-tuple-element.34), channel_id=1, source_target_pairs={{0,1},{1,2},{2,3},{4,5},{5,6},{6,7},{8,9},{9,10},{10,11},{12,13},{... | collective-permute-start | bytes 774152 | tf_op jit(solution)/shard_map/ppermute | solution.py:31
  183.9 11.4 %collective-permute-start.18 = (f32[7,1,18,512]{3,2,1,0:T(8,128)S(1)}, f32[7,1,18,512]{3,2,1,0:T(8,128)}, u32[]{:S(2)}, u32[]{:S(2)}) collective-permute-start(f32[7,1,18,512]{3,2,1,0:T(8,128)S(1)} %get-tuple-element.35), channel_id=1, source_target_pairs={{1,0},{2,1},{3,2},{5,4},{6,5},{7,6},{9,8},{10,9},{11,10},{13,12},{... | collective-permute-start | bytes 774152 | tf_op jit(solution)/shard_map/ppermute | solution.py:32
  (13 other events, 251.6 us)
where the time goes:
time: 200 us; the launch traced here: 199 us
  starting transfers between devices  95.8 us (48%)
  waiting for transfers between devices  43.7 us (22%)
  local copies, waits for them, and re-layouts  35.1 us (18%)
  other arithmetic  18.7 us (9%)
  matrix products  4.04 us (2%)
    all_to_all x4, starting transfers between devices, route_reply(): lax.all_to_all(crossed, 'ang', split_axis=1, concat_axis=1, tiled=True)  40 us
    ppermute x8, starting transfers between devices, padded(): before = lax.ppermute(last, axis, up)  25.4 us
    ppermute x8, waiting for transfers between devices, padded(): after = lax.ppermute(first, axis, down)  18.7 us
    ppermute x8, starting transfers between devices, padded(): after = lax.ppermute(first, axis, down)  16.8 us
    all_to_all x1, starting transfers between devices, route_request(): lax.all_to_all(crossed, 'ang', split_axis=0, concat_axis=0, tiled=True)  13.2 us
    gather x4, local copies, waits for them, and re-layouts, overset(): jnp.take(table, gather_index, axis=1).reshape(stacked_rows, slot_count, 4)  11.6 us
    reshape x4, local copies, waits for them, and re-layouts, overset(): table = current.reshape(stacked_rows, rows_p * rows_t)  10.7 us
    all_to_all x4, waiting for transfers between devices, route_reply(): lax.all_to_all(crossed, 'ang', split_axis=1, concat_axis=1, tiled=True)  10.4 us
  transfers between devices with their start and end apart: 26, of which 18 were waited for; matrix products, arithmetic and copies ran while one was open for 21% of the time, Pallas kernels for 0%

commit v1 on v0

--- a/solution.py
+++ b/solution.py
@@ -94,7 +94,10 @@
 
 def route_reply(answer):
     crossed = swapped(answer, "panel", 0)
-    return lax.all_to_all(crossed, "ang", split_axis=1, concat_axis=1, tiled=True)
+    return jnp.concatenate(
+        lax.all_to_all(jnp.stack(jnp.split(crossed, lax.axis_size("ang"), axis=1)), "ang", 0, 0),
+        axis=1,
+    )
 
 
 def body(

time: 200 us -> 271 us (1.35)
  local copies, waits for them, and re-layouts: 35.1 us -> 111 us
  waiting for transfers between devices: 43.7 us -> 38.4 us
    unnamed x54 -> x178, local copies, waits for them, and re-layouts: 3.45 us -> 77 us
    ppermute x5, waiting for transfers between devices: 6.01 us -> 1.49 us  [swapped(): return lax.ppermute(block, axis, route)]
  transfers between devices with their start and end apart: 26 -> 26, of which waited for: 18 -> 15; matrix products, arithmetic and copies ran while one was open for 21% -> 37% of each run, Pallas kernels for 0% -> 0%
where the time goes in v1:
time: 271 us; the launch traced here: 270 us
  local copies, waits for them, and re-layouts  111 us (41%)
  starting transfers between devices  95.8 us (35%)
  waiting for transfers between devices  38.4 us (14%)
  other arithmetic  18.7 us (7%)
  matrix products  4.04 us (1%)
    unnamed x178, local copies, waits for them, and re-layouts  77 us
    all_to_all x4, starting transfers between devices, route_reply(): lax.all_to_all(jnp.stack(jnp.split(crossed, lax.axis_size('ang'), axis=1)...  39.9 us
    ppermute x8, starting transfers between devices, padded(): before = lax.ppermute(last, axis, up)  25.2 us
    ppermute x8, waiting for transfers between devices, padded(): after = lax.ppermute(first, axis, down)  18.7 us
    ppermute x8, starting transfers between devices, padded(): after = lax.ppermute(first, axis, down)  17 us
    all_to_all x1, starting transfers between devices, route_request(): lax.all_to_all(crossed, 'ang', split_axis=0, concat_axis=0, tiled=True)  13.2 us
    gather x4, local copies, waits for them, and re-layouts, overset(): jnp.take(table, gather_index, axis=1).reshape(stacked_rows, slot_count, 4)  11.6 us
    reshape x4, local copies, waits for them, and re-layouts, overset(): table = current.reshape(stacked_rows, rows_p * rows_t)  10.7 us
  transfers between devices with their start and end apart: 26, of which 15 were waited for; matrix products, arithmetic and copies ran while one was open for 37% of the time, Pallas kernels for 0%

profile of v1, /device:TPU:2, one launch (start us, length us, event | category | flops | bytes accessed | tf_op | source)
XLA Modules:
  0.0 269.9 jit_solution(6122855452903727916)
XLA Ops:
  1.8 4.3 %collective-permute-start.1 = (f32[7,2,1,512]{3,2,1,0:T(1,128)S(1)}, f32[7,2,1,512]{3,2,1,0:T(1,128)S(1)}, u32[]{:S(2)}, u32[]{:S(2)}) collective-permute-start(f32[7,2,1,512]{3,2,1,0:T(1,128)S(1)} %get-tuple-element.75), channel_id=1, source_target_pairs={{4,0},{8,4},{12,8},{16,12},{20,16},{24,20},{28,24},{32,28},{36,32}... | collective-permute-start | bytes 86024 | tf_op jit(solution)/shard_map/ppermute | solution.py:32
  13.2 13.2 %all-to-all-start = ((f32[32,2,1]{1,2,0:T(1,128)}), f32[32,2,1]{1,2,0:T(1,128)S(1)}, u32[]{:S(2)}, u32[]{:S(2)}) async-start(f32[32,2,1]{1,2,0:T(1,128)} %copy.723), calls=%async_computation | async-start | bytes 32768 | tf_op jit(solution)/shard_map/all_to_all | solution.py:92
  30.2 4.7 %all-to-all-done = f32[32,2,1]{1,2,0:T(1,128)S(1)} async-done(((f32[32,2,1]{1,2,0:T(1,128)}), f32[32,2,1]{1,2,0:T(1,128)S(1)}, u32[]{:S(2)}, u32[]{:S(2)}) %all-to-all-start) | async-done | bytes 288 | tf_op jit(solution)/shard_map/all_to_all | solution.py:92
  35.3 2.9 %gather_fusion = f32[256,14]{1,0:T(8,128)S(1)} fusion(f32[14,8192]{0,1:T(8,128)} %copy.724, s32[1024]{0:T(1024)S(1)} %pad_clamp_fusion), kind=kCustom, calls=%fused_computation.clone | custom fusion | bytes 29696 | tf_op jit(solution)/shard_map/jit(_take)/gather | solution.py:158
  58.7 5.1 %all-to-all-start.1 = ((f32[32,14,1,2,4]{1,4,3,2,0:T(4,128)}), f32[32,14,1,2,4]{1,4,3,2,0:T(4,128)S(1)}, u32[]{:S(2)}, u32[]{:S(2)}) async-start(f32[32,14,1,2,4]{1,4,3,2,0:T(4,128)} %constant_dynamic-update-slice_fusion), calls=%async_computation.1 | async-start | bytes 262144 | tf_op jit(solution)/shard_map/all_to_all | solution.py:98
  65.3 4.2 %collective-permute-start.3 = (f32[7,1,18,512]{3,2,1,0:T(8,128)}, f32[7,1,18,512]{3,2,1,0:T(8,128)}, u32[]{:S(2)}, u32[]{:S(2)}) collective-permute-start(f32[7,1,18,512]{3,2,1,0:T(8,128)} %get-tuple-element.40), channel_id=1, source_target_pairs={{0,1},{1,2},{2,3},{4,5},{5,6},{6,7},{8,9},{9,10},{10,11},{12,13},{... | collective-permute-start | bytes 774152 | tf_op jit(solution)/shard_map/ppermute | solution.py:31
  76.3 4.6 %collective-permute-done.2 = f32[7,1,18,512]{3,2,1,0:T(8,128)} collective-permute-done((f32[7,1,18,512]{3,2,1,0:T(8,128)S(1)}, f32[7,1,18,512]{3,2,1,0:T(8,128)}, u32[]{:S(2)}, u32[]{:S(2)}) %collective-permute-start.2) | collective-permute-done | bytes 258080 | tf_op jit(solution)/shard_map/ppermute | solution.py:32
  86.3 2.9 %gather_fusion.1 = f32[256,14]{1,0:T(8,128)S(1)} fusion(f32[14,8192]{0,1:T(8,128)} %copy.734, s32[1024]{0:T(1024)S(1)} %pad_clamp_fusion), kind=kCustom, calls=%fused_computation.1.clone | custom fusion | bytes 29696 | tf_op jit(solution)/shard_map/jit(_take)/gather | solution.py:158
  92.0 3.3 %collective-permute-start.6 = (f32[7,2,1,512]{3,2,1,0:T(1,128)S(1)}, f32[7,2,1,512]{3,2,1,0:T(1,128)S(1)}, u32[]{:S(2)}, u32[]{:S(2)}) collective-permute-start(f32[7,2,1,512]{3,2,1,0:T(1,128)S(1)} %get-tuple-element.70), channel_id=1, source_target_pairs={{0,4},{4,8},{8,12},{12,16},{16,20},{20,24},{24,28},{28,32},{32,36}... | collective-permute-start | bytes 86024 | tf_op jit(solution)/shard_map/ppermute | solution.py:31
  114.3 11.7 %all-to-all-start.2 = ((f32[32,14,1,2,4]{1,4,3,2,0:T(4,128)}), f32[32,14,1,2,4]{1,4,3,2,0:T(4,128)S(1)}, u32[]{:S(2)}, u32[]{:S(2)}) async-start(f32[32,14,1,2,4]{1,4,3,2,0:T(4,128)} %constant_dynamic-update-slice_fusion.60), calls=%async_computation.2 | async-start | bytes 262144 | tf_op jit(solution)/shard_map/all_to_all | solution.py:98
  127.6 3.5 %collective-permute-start.9 = (f32[7,1,18,512]{3,2,1,0:T(8,128)}, f32[7,1,18,512]{3,2,1,0:T(8,128)}, u32[]{:S(2)}, u32[]{:S(2)}) collective-permute-start(f32[7,1,18,512]{3,2,1,0:T(8,128)} %get-tuple-element.38), channel_id=1, source_target_pairs={{0,1},{1,2},{2,3},{4,5},{5,6},{6,7},{8,9},{9,10},{10,11},{12,13},{... | collective-permute-start | bytes 774152 | tf_op jit(solution)/shard_map/ppermute | solution.py:31
  137.5 4.8 %collective-permute-done.8 = f32[7,1,18,512]{3,2,1,0:T(8,128)} collective-permute-done((f32[7,1,18,512]{3,2,1,0:T(8,128)}, f32[7,1,18,512]{3,2,1,0:T(8,128)}, u32[]{:S(2)}, u32[]{:S(2)}) %collective-permute-start.8) | collective-permute-done | bytes 258080 | tf_op jit(solution)/shard_map/ppermute | solution.py:32
  146.4 2.7 copy.744
  149.1 2.9 %gather_fusion.2 = f32[256,14]{1,0:T(8,128)S(1)} fusion(f32[14,8192]{0,1:T(8,128)} %copy.744, s32[1024]{0:T(1024)S(1)} %pad_clamp_fusion), kind=kCustom, calls=%fused_computation.2.clone | custom fusion | bytes 29696 | tf_op jit(solution)/shard_map/jit(_take)/gather | solution.py:158
  154.7 3.4 %collective-permute-start.11 = (f32[7,2,1,512]{3,2,1,0:T(1,128)S(1)}, f32[7,2,1,512]{3,2,1,0:T(1,128)S(1)}, u32[]{:S(2)}, u32[]{:S(2)}) collective-permute-start(f32[7,2,1,512]{3,2,1,0:T(1,128)S(1)} %get-tuple-element.66), channel_id=1, source_target_pairs={{0,4},{4,8},{8,12},{12,16},{16,20},{20,24},{24,28},{28,32},{32,36}... | collective-permute-start | bytes 86024 | tf_op jit(solution)/shard_map/ppermute | solution.py:31
  177.1 11.6 %all-to-all-start.3 = ((f32[32,14,1,2,4]{1,4,3,2,0:T(4,128)}), f32[32,14,1,2,4]{1,4,3,2,0:T(4,128)S(1)}, u32[]{:S(2)}, u32[]{:S(2)}) async-start(f32[32,14,1,2,4]{1,4,3,2,0:T(4,128)} %constant_dynamic-update-slice_fusion.120), calls=%async_computation.3 | async-start | bytes 262144 | tf_op jit(solution)/shard_map/all_to_all | solution.py:98
  191.0 3.2 %collective-permute-start.14 = (f32[7,1,18,512]{3,2,1,0:T(8,128)}, f32[7,1,18,512]{3,2,1,0:T(8,128)}, u32[]{:S(2)}, u32[]{:S(2)}) collective-permute-start(f32[7,1,18,512]{3,2,1,0:T(8,128)} %get-tuple-element.36), channel_id=1, source_target_pairs={{0,1},{1,2},{2,3},{4,5},{5,6},{6,7},{8,9},{9,10},{10,11},{12,13},{... | collective-permute-start | bytes 774152 | tf_op jit(solution)/shard_map/ppermute | solution.py:31
  200.7 4.6 %collective-permute-done.13 = f32[7,1,18,512]{3,2,1,0:T(8,128)} collective-permute-done((f32[7,1,18,512]{3,2,1,0:T(8,128)S(1)}, f32[7,1,18,512]{3,2,1,0:T(8,128)}, u32[]{:S(2)}, u32[]{:S(2)}) %collective-permute-start.13) | collective-permute-done | bytes 258080 | tf_op jit(solution)/shard_map/ppermute | solution.py:32
  208.0 2.7 copy.754
  210.7 2.9 %gather_fusion.3 = f32[256,14]{1,0:T(8,128)S(1)} fusion(f32[14,8192]{0,1:T(8,128)} %copy.754, s32[1024]{0:T(1024)S(1)} %pad_clamp_fusion), kind=kCustom, calls=%fused_computation.3.clone | custom fusion | bytes 29696 | tf_op jit(solution)/shard_map/jit(_take)/gather | solution.py:158
  216.3 3.4 %collective-permute-start.16 = (f32[7,2,1,512]{3,2,1,0:T(1,128)S(1)}, f32[7,2,1,512]{3,2,1,0:T(1,128)S(1)}, u32[]{:S(2)}, u32[]{:S(2)}) collective-permute-start(f32[7,2,1,512]{3,2,1,0:T(1,128)S(1)} %get-tuple-element.62), channel_id=1, source_target_pairs={{0,4},{4,8},{8,12},{12,16},{16,20},{20,24},{24,28},{28,32},{32,36}... | collective-permute-start | bytes 86024 | tf_op jit(solution)/shard_map/ppermute | solution.py:31
  238.7 11.6 %all-to-all-start.4 = ((f32[32,14,1,2,4]{1,4,3,2,0:T(4,128)}), f32[32,14,1,2,4]{1,4,3,2,0:T(4,128)S(1)}, u32[]{:S(2)}, u32[]{:S(2)}) async-start(f32[32,14,1,2,4]{1,4,3,2,0:T(4,128)} %constant_dynamic-update-slice_fusion.180), calls=%async_computation.4 | async-start | bytes 262144 | tf_op jit(solution)/shard_map/all_to_all | solution.py:98
  256.1 3.1 %all-to-all-done.4 = f32[32,14,1,2,4]{1,4,3,2,0:T(4,128)S(1)} async-done(((f32[32,14,1,2,4]{1,4,3,2,0:T(4,128)}), f32[32,14,1,2,4]{1,4,3,2,0:T(4,128)S(1)}, u32[]{:S(2)}, u32[]{:S(2)}) %all-to-all-start.4) | async-done | bytes 14368 | tf_op jit(solution)/shard_map/all_to_all | solution.py:98
  261.3 4.6 %collective-permute-done.18 = f32[7,1,18,512]{3,2,1,0:T(8,128)} collective-permute-done((f32[7,1,18,512]{3,2,1,0:T(8,128)S(1)}, f32[7,1,18,512]{3,2,1,0:T(8,128)}, u32[]{:S(2)}, u32[]{:S(2)}) %collective-permute-start.18) | collective-permute-done | bytes 258080 | tf_op jit(solution)/shard_map/ppermute | solution.py:32
  (398 shorter events, 145.8 us)
Async XLA Ops:
  1.8 62.0 %collective-permute-start.1 = (f32[7,2,1,512]{3,2,1,0:T(1,128)S(1)}, f32[7,2,1,512]{3,2,1,0:T(1,128)S(1)}, u32[]{:S(2)}, u32[]{:S(2)}) collective-permute-start(f32[7,2,1,512]{3,2,1,0:T(1,128)S(1)} %get-tuple-element.75), channel_id=1, source_target_pairs={{4,0},{8,4},{12,8},{16,12},{20,16},{24,20},{28,24},{32,28},{36,32}... | collective-permute-start | bytes 86024 | tf_op jit(solution)/shard_map/ppermute | solution.py:32
  6.1 57.7 %collective-permute-start = (f32[7,2,1,512]{3,2,1,0:T(1,128)S(1)}, f32[7,2,1,512]{3,2,1,0:T(1,128)S(1)}, u32[]{:S(2)}, u32[]{:S(2)}) collective-permute-start(f32[7,2,1,512]{3,2,1,0:T(1,128)S(1)} %get-tuple-element.74), channel_id=1, source_target_pairs={{0,4},{4,8},{8,12},{12,16},{16,20},{20,24},{24,28},{28,32},{32,36}... | collective-permute-start | bytes 86024 | tf_op jit(solution)/shard_map/ppermute | solution.py:31
  13.2 21.7 %all-to-all-start = ((f32[32,2,1]{1,2,0:T(1,128)}), f32[32,2,1]{1,2,0:T(1,128)S(1)}, u32[]{:S(2)}, u32[]{:S(2)}) async-start(f32[32,2,1]{1,2,0:T(1,128)} %copy.723), calls=%async_computation | async-start | bytes 32768 | tf_op jit(solution)/shard_map/all_to_all | solution.py:92
  58.7 14.2 %all-to-all-start.1 = ((f32[32,14,1,2,4]{1,4,3,2,0:T(4,128)}), f32[32,14,1,2,4]{1,4,3,2,0:T(4,128)S(1)}, u32[]{:S(2)}, u32[]{:S(2)}) async-start(f32[32,14,1,2,4]{1,4,3,2,0:T(4,128)} %constant_dynamic-update-slice_fusion), calls=%async_computation.1 | async-start | bytes 262144 | tf_op jit(solution)/shard_map/all_to_all | solution.py:98
  65.3 11.0 %collective-permute-start.3 = (f32[7,1,18,512]{3,2,1,0:T(8,128)}, f32[7,1,18,512]{3,2,1,0:T(8,128)}, u32[]{:S(2)}, u32[]{:S(2)}) collective-permute-start(f32[7,1,18,512]{3,2,1,0:T(8,128)} %get-tuple-element.40), channel_id=1, source_target_pairs={{0,1},{1,2},{2,3},{4,5},{5,6},{6,7},{8,9},{9,10},{10,11},{12,13},{... | collective-permute-start | bytes 774152 | tf_op jit(solution)/shard_map/ppermute | solution.py:31
  69.5 11.4 %collective-permute-start.2 = (f32[7,1,18,512]{3,2,1,0:T(8,128)S(1)}, f32[7,1,18,512]{3,2,1,0:T(8,128)}, u32[]{:S(2)}, u32[]{:S(2)}) collective-permute-start(f32[7,1,18,512]{3,2,1,0:T(8,128)S(1)} %get-tuple-element.41), channel_id=1, source_target_pairs={{1,0},{2,1},{3,2},{5,4},{6,5},{7,6},{9,8},{10,9},{11,10},{13,12},{... | collective-permute-start | bytes 774152 | tf_op jit(solution)/shard_map/ppermute | solution.py:32
  89.3 6.0 %collective-permute-start.10 = (f32[14,32,2,4]{0,3,2,1:T(4,128)S(1)}, f32[14,32,2,4]{0,3,2,1:T(4,128)S(1)}, u32[]{:S(2)}, u32[]{:S(2)}) collective-permute-start(f32[14,32,2,4]{0,3,2,1:T(4,128)S(1)} %bitcast.788), channel_id=1, source_target_pairs={{0,128},{128,0},{1,129},{129,1},{2,130},{130,2},{3,131},{131,3},{4... | collective-permute-start | bytes 43016 | tf_op jit(solution)/shard_map/ppermute | solution.py:21
  89.5 36.6 %collective-permute-start.7 = (f32[7,2,1,512]{3,2,1,0:T(1,128)S(1)}, f32[7,2,1,512]{3,2,1,0:T(1,128)S(1)}, u32[]{:S(2)}, u32[]{:S(2)}) collective-permute-start(f32[7,2,1,512]{3,2,1,0:T(1,128)S(1)} %get-tuple-element.71), channel_id=1, source_target_pairs={{4,0},{8,4},{12,8},{16,12},{20,16},{24,20},{28,24},{32,28},{36,32}... | collective-permute-start | bytes 86024 | tf_op jit(solution)/shard_map/ppermute | solution.py:32
  92.0 34.0 %collective-permute-start.6 = (f32[7,2,1,512]{3,2,1,0:T(1,128)S(1)}, f32[7,2,1,512]{3,2,1,0:T(1,128)S(1)}, u32[]{:S(2)}, u32[]{:S(2)}) collective-permute-start(f32[7,2,1,512]{3,2,1,0:T(1,128)S(1)} %get-tuple-element.70), channel_id=1, source_target_pairs={{0,4},{4,8},{8,12},{12,16},{16,20},{20,24},{24,28},{28,32},{32,36}... | collective-permute-start | bytes 86024 | tf_op jit(solution)/shard_map/ppermute | solution.py:31
  114.3 20.6 %all-to-all-start.2 = ((f32[32,14,1,2,4]{1,4,3,2,0:T(4,128)}), f32[32,14,1,2,4]{1,4,3,2,0:T(4,128)S(1)}, u32[]{:S(2)}, u32[]{:S(2)}) async-start(f32[32,14,1,2,4]{1,4,3,2,0:T(4,128)} %constant_dynamic-update-slice_fusion.60), calls=%async_computation.2 | async-start | bytes 262144 | tf_op jit(solution)/shard_map/all_to_all | solution.py:98
  127.6 9.9 %collective-permute-start.9 = (f32[7,1,18,512]{3,2,1,0:T(8,128)}, f32[7,1,18,512]{3,2,1,0:T(8,128)}, u32[]{:S(2)}, u32[]{:S(2)}) collective-permute-start(f32[7,1,18,512]{3,2,1,0:T(8,128)} %get-tuple-element.38), channel_id=1, source_target_pairs={{0,1},{1,2},{2,3},{4,5},{5,6},{6,7},{8,9},{9,10},{10,11},{12,13},{... | collective-permute-start | bytes 774152 | tf_op jit(solution)/shard_map/ppermute | solution.py:31
  131.1 11.3 %collective-permute-start.8 = (f32[7,1,18,512]{3,2,1,0:T(8,128)}, f32[7,1,18,512]{3,2,1,0:T(8,128)}, u32[]{:S(2)}, u32[]{:S(2)}) collective-permute-start(f32[7,1,18,512]{3,2,1,0:T(8,128)} %get-tuple-element.39), channel_id=1, source_target_pairs={{1,0},{2,1},{3,2},{5,4},{6,5},{7,6},{9,8},{10,9},{11,10},{13,12},{... | collective-permute-start | bytes 774152 | tf_op jit(solution)/shard_map/ppermute | solution.py:32
  152.1 6.0 %collective-permute-start.15 = (f32[14,32,2,4]{0,3,2,1:T(4,128)S(1)}, f32[14,32,2,4]{0,3,2,1:T(4,128)S(1)}, u32[]{:S(2)}, u32[]{:S(2)}) collective-permute-start(f32[14,32,2,4]{0,3,2,1:T(4,128)S(1)} %bitcast.789), channel_id=1, source_target_pairs={{0,128},{128,0},{1,129},{129,1},{2,130},{130,2},{3,131},{131,3},{4... | collective-permute-start | bytes 43016 | tf_op jit(solution)/shard_map/ppermute | solution.py:21
  152.2 36.5 %collective-permute-start.12 = (f32[7,2,1,512]{3,2,1,0:T(1,128)S(1)}, f32[7,2,1,512]{3,2,1,0:T(1,128)S(1)}, u32[]{:S(2)}, u32[]{:S(2)}) collective-permute-start(f32[7,2,1,512]{3,2,1,0:T(1,128)S(1)} %get-tuple-element.67), channel_id=1, source_target_pairs={{4,0},{8,4},{12,8},{16,12},{20,16},{24,20},{28,24},{32,28},{36,32}... | collective-permute-start | bytes 86024 | tf_op jit(solution)/shard_map/ppermute | solution.py:32
  154.7 34.0 %collective-permute-start.11 = (f32[7,2,1,512]{3,2,1,0:T(1,128)S(1)}, f32[7,2,1,512]{3,2,1,0:T(1,128)S(1)}, u32[]{:S(2)}, u32[]{:S(2)}) collective-permute-start(f32[7,2,1,512]{3,2,1,0:T(1,128)S(1)} %get-tuple-element.66), channel_id=1, source_target_pairs={{0,4},{4,8},{8,12},{12,16},{16,20},{20,24},{24,28},{28,32},{32,36}... | collective-permute-start | bytes 86024 | tf_op jit(solution)/shard_map/ppermute | solution.py:31
  177.1 20.5 %all-to-all-start.3 = ((f32[32,14,1,2,4]{1,4,3,2,0:T(4,128)}), f32[32,14,1,2,4]{1,4,3,2,0:T(4,128)S(1)}, u32[]{:S(2)}, u32[]{:S(2)}) async-start(f32[32,14,1,2,4]{1,4,3,2,0:T(4,128)} %constant_dynamic-update-slice_fusion.120), calls=%async_computation.3 | async-start | bytes 262144 | tf_op jit(solution)/shard_map/all_to_all | solution.py:98
  191.0 9.6 %collective-permute-start.14 = (f32[7,1,18,512]{3,2,1,0:T(8,128)}, f32[7,1,18,512]{3,2,1,0:T(8,128)}, u32[]{:S(2)}, u32[]{:S(2)}) collective-permute-start(f32[7,1,18,512]{3,2,1,0:T(8,128)} %get-tuple-element.36), channel_id=1, source_target_pairs={{0,1},{1,2},{2,3},{4,5},{5,6},{6,7},{8,9},{9,10},{10,11},{12,13},{... | collective-permute-start | bytes 774152 | tf_op jit(solution)/shard_map/ppermute | solution.py:31
  194.2 11.0 %collective-permute-start.13 = (f32[7,1,18,512]{3,2,1,0:T(8,128)S(1)}, f32[7,1,18,512]{3,2,1,0:T(8,128)}, u32[]{:S(2)}, u32[]{:S(2)}) collective-permute-start(f32[7,1,18,512]{3,2,1,0:T(8,128)S(1)} %get-tuple-element.37), channel_id=1, source_target_pairs={{1,0},{2,1},{3,2},{5,4},{6,5},{7,6},{9,8},{10,9},{11,10},{13,12},{... | collective-permute-start | bytes 774152 | tf_op jit(solution)/shard_map/ppermute | solution.py:32
  213.7 6.0 %collective-permute-start.20 = (f32[14,32,2,4]{0,3,2,1:T(4,128)S(1)}, f32[14,32,2,4]{0,3,2,1:T(4,128)S(1)}, u32[]{:S(2)}, u32[]{:S(2)}) collective-permute-start(f32[14,32,2,4]{0,3,2,1:T(4,128)S(1)} %bitcast.787), channel_id=1, source_target_pairs={{0,128},{128,0},{1,129},{129,1},{2,130},{130,2},{3,131},{131,3},{4... | collective-permute-start | bytes 43016 | tf_op jit(solution)/shard_map/ppermute | solution.py:21
  213.8 36.5 %collective-permute-start.17 = (f32[7,2,1,512]{3,2,1,0:T(1,128)S(1)}, f32[7,2,1,512]{3,2,1,0:T(1,128)S(1)}, u32[]{:S(2)}, u32[]{:S(2)}) collective-permute-start(f32[7,2,1,512]{3,2,1,0:T(1,128)S(1)} %get-tuple-element.63), channel_id=1, source_target_pairs={{4,0},{8,4},{12,8},{16,12},{20,16},{24,20},{28,24},{32,28},{36,32}... | collective-permute-start | bytes 86024 | tf_op jit(solution)/shard_map/ppermute | solution.py:32
  216.3 34.0 %collective-permute-start.16 = (f32[7,2,1,512]{3,2,1,0:T(1,128)S(1)}, f32[7,2,1,512]{3,2,1,0:T(1,128)S(1)}, u32[]{:S(2)}, u32[]{:S(2)}) collective-permute-start(f32[7,2,1,512]{3,2,1,0:T(1,128)S(1)} %get-tuple-element.62), channel_id=1, source_target_pairs={{0,4},{4,8},{8,12},{12,16},{16,20},{20,24},{24,28},{28,32},{32,36}... | collective-permute-start | bytes 86024 | tf_op jit(solution)/shard_map/ppermute | solution.py:31
  238.7 20.5 %all-to-all-start.4 = ((f32[32,14,1,2,4]{1,4,3,2,0:T(4,128)}), f32[32,14,1,2,4]{1,4,3,2,0:T(4,128)S(1)}, u32[]{:S(2)}, u32[]{:S(2)}) async-start(f32[32,14,1,2,4]{1,4,3,2,0:T(4,128)} %constant_dynamic-update-slice_fusion.180), calls=%async_computation.4 | async-start | bytes 262144 | tf_op jit(solution)/shard_map/all_to_all | solution.py:98
  252.6 8.7 %collective-permute-start.19 = (f32[7,1,18,512]{3,2,1,0:T(8,128)}, f32[7,1,18,512]{3,2,1,0:T(8,128)}, u32[]{:S(2)}, u32[]{:S(2)}) collective-permute-start(f32[7,1,18,512]{3,2,1,0:T(8,128)} %get-tuple-element.34), channel_id=1, source_target_pairs={{0,1},{1,2},{2,3},{4,5},{5,6},{6,7},{8,9},{9,10},{10,11},{12,13},{... | collective-permute-start | bytes 774152 | tf_op jit(solution)/shard_map/ppermute | solution.py:31
  254.8 11.1 %collective-permute-start.18 = (f32[7,1,18,512]{3,2,1,0:T(8,128)S(1)}, f32[7,1,18,512]{3,2,1,0:T(8,128)}, u32[]{:S(2)}, u32[]{:S(2)}) collective-permute-start(f32[7,1,18,512]{3,2,1,0:T(8,128)S(1)} %get-tuple-element.35), channel_id=1, source_target_pairs={{1,0},{2,1},{3,2},{5,4},{6,5},{7,6},{9,8},{10,9},{11,10},{13,12},{... | collective-permute-start | bytes 774152 | tf_op jit(solution)/shard_map/ppermute | solution.py:32
  (13 other events, 325.5 us)
